TPU v7x, 32 devices: a whole 2x2x4 slice. The times are simulated.
32 devices in a mesh: dp: 16 (over z, y, x), mp: 2 (over core).
Axes of the slice: x: 2, y: 2, z: 4, core: 2. Of those that a mesh axis runs over, the one named last changes fastest.
Arguments:
- tokens: bfloat16 [32768, 768], P('dp'), may hold values from -6 to 6
- cond: bfloat16 [32768, 128], P('dp'), may hold values from -6 to 6
- segments: int32 [32, 1024], P('dp'), may hold values from 0 to 3, never falling along the last dimension, each value on 1 to 512 neighbouring positions
- out_grad: bfloat16 [32768, 768], P('dp'), may hold values from -6 to 6
- step: int32 [1], replicated, may hold values from 2 to 20
- ada_weight: float32 [128, 4608], P(None, 'dp'), may hold values from -0.5 to 0.5
- ada_first: float32 [128, 4608], P(None, 'dp'), may hold values from -0.00061035156 to 0.00061035156
- ada_second: float32 [128, 4608], P(None, 'dp'), may hold values from 1.3031258e-10 to 5.212503e-10
- norm_params: float32 [8, 768], P(None, 'dp'), may hold values from 0.5 to 1.5
- norm_first: float32 [8, 768], P(None, 'dp'), may hold values from -0.0024414062 to 0.0024414062
- norm_second: float32 [8, 768], P(None, 'dp'), may hold values from 2.6062516e-10 to 1.0425006e-09
- qkv_weight: float32 [3, 768, 768], P(None, 'dp', 'mp'), may hold values from -0.109375 to 0.109375
- qkv_first: float32 [3, 768, 768], P(None, 'dp', 'mp'), may hold values from -0.00061035156 to 0.00061035156
- qkv_second: float32 [3, 768, 768], P(None, 'dp', 'mp'), may hold values from 1.3031258e-10 to 5.212503e-10
- out_weight: float32 [768, 768], P('mp', 'dp'), may hold values from -1.75 to 1.75
- out_first: float32 [768, 768], P('mp', 'dp'), may hold values from -0.00061035156 to 0.00061035156
- out_second: float32 [768, 768], P('mp', 'dp'), may hold values from 1.6289073e-11 to 6.515629e-11
- up_weight: float32 [768, 3072], P('dp', 'mp'), may hold values from -0.21875 to 0.21875
- up_first: float32 [768, 3072], P('dp', 'mp'), may hold values from -0.00061035156 to 0.00061035156
- up_second: float32 [768, 3072], P('dp', 'mp'), may hold values from 1.3031258e-10 to 5.212503e-10
- down_weight: float32 [3072, 768], P('mp', 'dp'), may hold values from -0.109375 to 0.109375
- down_first: float32 [3072, 768], P('mp', 'dp'), may hold values from -0.00061035156 to 0.00061035156
- down_second: float32 [3072, 768], P('mp', 'dp'), may hold values from 1.3031258e-10 to 5.212503e-10
Outputs:
- result: bfloat16 [32768, 768], P('dp')
- input_grad: float32 [32768, 768], P('dp')
- grad_norm: float32 [1], replicated
- ada_weight_next: float32 [128, 4608], P(None, 'dp')
- ada_first_next: float32 [128, 4608], P(None, 'dp')
- ada_second_next: float32 [128, 4608], P(None, 'dp')
- norm_params_next: float32 [8, 768], P(None, 'dp')
- norm_first_next: float32 [8, 768], P(None, 'dp')
- norm_second_next: float32 [8, 768], P(None, 'dp')
- qkv_weight_next: float32 [3, 768, 768], P(None, 'dp', 'mp')
- qkv_first_next: float32 [3, 768, 768], P(None, 'dp', 'mp')
- qkv_second_next: float32 [3, 768, 768], P(None, 'dp', 'mp')
- out_weight_next: float32 [768, 768], P('mp', 'dp')
- out_first_next: float32 [768, 768], P('mp', 'dp')
- out_second_next: float32 [768, 768], P('mp', 'dp')
- up_weight_next: float32 [768, 3072], P('dp', 'mp')
- up_first_next: float32 [768, 3072], P('dp', 'mp')
- up_second_next: float32 [768, 3072], P('dp', 'mp')
- down_weight_next: float32 [3072, 768], P('mp', 'dp')
- down_first_next: float32 [3072, 768], P('mp', 'dp')
- down_second_next: float32 [3072, 768], P('mp', 'dp')
Inputs may be any that keep to these rules, and one draw needn't show every extreme that they name: `segments`: along each sequence document ids never fall; each document holds 1 to 512 positions, and one document of a sequence holds exactly 512.
All inputs are finite; a program needn't handle non-finite values.
Results may differ from a plain program's by a relative error of at most 0.012.
The roundings to bfloat16 on the way count: a program that leaves them out, or rounds other values in their place, can miss the bound.
Values may be sent and summed in bfloat16 or wider, within the bound.
A program may use at most 320 MiB of HBM per device.

v0:
```python
import math
import jax
import jax.numpy as jnp
from jax import lax
from jax.sharding import PartitionSpec as P

HEAD_DIM = 64
clip_limit = 1.0
step_rates = (0.075, 0.75, 0.075, 0.25, 0.075, 0.075)
decay_rates = (0.01, 0.0, 0.01, 0.01, 0.01, 0.01)


def modnorm(inputs, gain_row, shift_row, scale_row):
    centre = inputs - jnp.mean(inputs, axis=-1, keepdims=True)
    spread = jnp.mean(centre * centre, axis=-1, keepdims=True)
    return centre * lax.rsqrt(spread + 1e-05) * gain_row * (1.0 + scale_row) + shift_row


def rope_tables(length, head_size):
    half_dim = head_size // 2
    inverse = jnp.exp(
        jnp.arange(half_dim, dtype=jnp.float32) * (-2.0 * math.log(10000.0) / head_size)
    )
    angles = jnp.arange(length, dtype=jnp.float32)[:, None] * inverse[None, :]
    return (jnp.cos(angles), jnp.sin(angles))


def rotate(values, cosines, sines):
    half_dim = values.shape[-1] // 2
    first_half = values[..., :half_dim]
    second_half = values[..., half_dim:]
    cos_row = cosines[:, None, :]
    sin_row = sines[:, None, :]
    return jnp.concatenate(
        [
            first_half * cos_row - second_half * sin_row,
            second_half * cos_row + first_half * sin_row,
        ],
        axis=-1,
    )


def unrotate(grads, cosines, sines):
    half_dim = grads.shape[-1] // 2
    first_half = grads[..., :half_dim]
    second_half = grads[..., half_dim:]
    cos_row = cosines[:, None, :]
    sin_row = sines[:, None, :]
    return jnp.concatenate(
        [
            first_half * cos_row + second_half * sin_row,
            second_half * cos_row - first_half * sin_row,
        ],
        axis=-1,
    )


def gelu_tanh(values):
    return jax.nn.gelu(values, approximate=True)


def adam_update(
    weight, first_moment, second_moment, grad_mean, clip_factor, step_count, step_rate, decay_rate
):
    clipped = grad_mean * clip_factor
    first_new = 0.9 * first_moment + 0.1 * clipped
    second_new = 0.999 * second_moment + 0.001 * clipped * clipped
    fix_one = 1.0 - jnp.exp(step_count * math.log(0.9))
    fix_two = 1.0 - jnp.exp(step_count * math.log(0.999))
    update = first_new / fix_one / (jnp.sqrt(second_new / fix_two) + 1e-08) + decay_rate * weight
    return (weight - step_rate * update, first_new, second_new)


def per_device(
    tokens,
    cond,
    segments,
    out_grad,
    step,
    ada_weight,
    ada_first,
    ada_second,
    norm_params,
    norm_first,
    norm_second,
    qkv_weight,
    qkv_first,
    qkv_second,
    out_weight,
    out_first,
    out_second,
    up_weight,
    up_first,
    up_second,
    down_weight,
    down_first,
    down_second,
):
    ada_low, norm_low, qkv_low, out_low, up_low, down_low = (
        lax.all_gather(ada_weight.astype(jnp.bfloat16), "dp", axis=1, tiled=True),
        lax.all_gather(norm_params.astype(jnp.bfloat16), "dp", axis=1, tiled=True),
        lax.all_gather(qkv_weight.astype(jnp.bfloat16), "dp", axis=1, tiled=True),
        lax.all_gather(out_weight.astype(jnp.bfloat16), "dp", axis=1, tiled=True),
        lax.all_gather(up_weight.astype(jnp.bfloat16), "dp", axis=0, tiled=True),
        lax.all_gather(down_weight.astype(jnp.bfloat16), "dp", axis=1, tiled=True),
    )
    model_width = norm_low.shape[1]
    tok_rows = tokens.shape[0]
    seq_count = segments.shape[0]
    seq_length = segments.shape[1]
    heads_local = qkv_low.shape[2] // HEAD_DIM
    score_scale = HEAD_DIM ** (-0.5)
    cosines, sines = rope_tables(seq_length, HEAD_DIM)
    inputs = tokens.astype(jnp.float32)
    cond_low = jax.nn.silu(cond.astype(jnp.float32)).astype(jnp.bfloat16)
    norm_vals = norm_low.astype(jnp.float32)
    modulation = jnp.dot(cond_low, ada_low, preferred_element_type=jnp.float32) + norm_vals[
        2:
    ].reshape(-1)
    shift_one = modulation[:, 0:model_width]
    scale_one = modulation[:, model_width : 2 * model_width]
    gate_one = modulation[:, 2 * model_width : 3 * model_width]
    shift_two = modulation[:, 3 * model_width : 4 * model_width]
    scale_two = modulation[:, 4 * model_width : 5 * model_width]
    gate_two = modulation[:, 5 * model_width : 6 * model_width]
    h_one = modnorm(inputs, norm_vals[0], shift_one, scale_one).astype(jnp.bfloat16)
    projected = jnp.einsum("td,cde->cte", h_one, qkv_low, preferred_element_type=jnp.float32)
    shaped = projected.reshape(3, seq_count, seq_length, heads_local, HEAD_DIM)
    queries = rotate(shaped[0], cosines, sines).astype(jnp.bfloat16)
    keys = rotate(shaped[1], cosines, sines).astype(jnp.bfloat16)
    values = shaped[2].astype(jnp.bfloat16)

    def scores_of(query_block, key_block, segment_row):
        raw_scores = jnp.einsum(
            "qhd,khd->hqk", query_block, key_block, preferred_element_type=jnp.float32
        )
        same_doc = segment_row[:, None] == segment_row[None, :]
        return jnp.where(same_doc[None], raw_scores * score_scale, -1e30)

    def attend(packed):
        query_block, key_block, value_block, segment_row = packed
        scores = scores_of(query_block, key_block, segment_row)
        row_top = jnp.max(scores, axis=-1, keepdims=True)
        row_total = jnp.sum(jnp.exp(scores - row_top), axis=-1, keepdims=True)
        logsum = row_top + jnp.log(row_total)
        softmax_w = jnp.exp(scores - logsum).astype(jnp.bfloat16)
        mixed_out = jnp.einsum(
            "hqk,khd->qhd", softmax_w, value_block, preferred_element_type=jnp.float32
        )
        return (mixed_out.astype(jnp.bfloat16), logsum)

    attended, logsums = lax.map(attend, (queries, keys, values, segments))
    attn_flat = attended.reshape(tok_rows, -1)
    attn_part = jnp.dot(attn_flat, out_low, preferred_element_type=jnp.float32)
    branch = lax.psum(attn_part, "mp")
    middle = inputs + gate_one * branch
    h_two = modnorm(middle, norm_vals[1], shift_two, scale_two).astype(jnp.bfloat16)
    hidden_pre = jnp.dot(h_two, up_low, preferred_element_type=jnp.float32)
    hidden = gelu_tanh(hidden_pre).astype(jnp.bfloat16)
    mlp_part = jnp.dot(hidden, down_low, preferred_element_type=jnp.float32)
    cotangent = out_grad.astype(jnp.float32)
    mlp_out = lax.psum(mlp_part, "mp")
    result = (middle + gate_two * mlp_out).astype(jnp.bfloat16)
    d_gate_two = cotangent * mlp_out
    mlp_grad = (gate_two * cotangent).astype(jnp.bfloat16)
    grad_down = jnp.einsum("tf,td->fd", hidden, mlp_grad, preferred_element_type=jnp.float32)
    grad_hidden = jnp.einsum("td,fd->tf", mlp_grad, down_low, preferred_element_type=jnp.float32)
    unused_gelu, gelu_back = jax.vjp(gelu_tanh, hidden_pre)
    grad_pre = gelu_back(grad_hidden)[0].astype(jnp.bfloat16)
    grad_up = jnp.einsum("td,tf->df", h_two, grad_pre, preferred_element_type=jnp.float32)
    h_two_part = jnp.einsum("tf,df->td", grad_pre, up_low, preferred_element_type=jnp.float32)
    h_two_grad = lax.psum(h_two_part, "mp")
    unused_two, norm_two_back = jax.vjp(modnorm, middle, norm_vals[1], shift_two, scale_two)
    d_middle, d_gain_two, d_shift_two, d_scale_two = norm_two_back(h_two_grad)
    middle_grad = cotangent + d_middle
    attn_grad = (gate_one * middle_grad).astype(jnp.bfloat16)
    d_gate_one = middle_grad * branch
    grad_out = jnp.einsum("te,td->ed", attn_flat, attn_grad, preferred_element_type=jnp.float32)
    out_back = jnp.einsum(
        "td,ed->te", attn_grad, out_low, preferred_element_type=jnp.float32
    ).astype(jnp.bfloat16)
    grad_attended = out_back.reshape(seq_count, seq_length, heads_local, HEAD_DIM)

    def attend_back(packed):
        query_block, key_block, value_block, segment_row, logsum, upstream = packed
        scores = scores_of(query_block, key_block, segment_row)
        softmax_w = jnp.exp(scores - logsum)
        grad_weights = jnp.einsum(
            "qhd,khd->hqk", upstream, value_block, preferred_element_type=jnp.float32
        )
        grad_value = jnp.einsum(
            "hqk,qhd->khd",
            softmax_w.astype(jnp.bfloat16),
            upstream,
            preferred_element_type=jnp.float32,
        )
        row_delta = jnp.sum(softmax_w * grad_weights, axis=-1, keepdims=True)
        grad_scores = (softmax_w * (grad_weights - row_delta) * score_scale).astype(jnp.bfloat16)
        grad_query = jnp.einsum(
            "hqk,khd->qhd", grad_scores, key_block, preferred_element_type=jnp.float32
        )
        grad_key = jnp.einsum(
            "hqk,qhd->khd", grad_scores, query_block, preferred_element_type=jnp.float32
        )
        return (grad_query, grad_key, grad_value)

    grad_q, grad_k, grad_v = lax.map(
        attend_back, (queries, keys, values, segments, logsums, grad_attended)
    )
    grad_proj = (
        jnp.stack([unrotate(grad_q, cosines, sines), unrotate(grad_k, cosines, sines), grad_v])
        .reshape(3, tok_rows, -1)
        .astype(jnp.bfloat16)
    )
    grad_qkv = jnp.einsum("td,cte->cde", h_one, grad_proj, preferred_element_type=jnp.float32)
    h_one_part = jnp.einsum("cte,cde->td", grad_proj, qkv_low, preferred_element_type=jnp.float32)
    h_one_grad = lax.psum(h_one_part, "mp")
    unused_one, norm_one_back = jax.vjp(modnorm, inputs, norm_vals[0], shift_one, scale_one)
    d_inputs, d_gain_one, d_shift_one, d_scale_one = norm_one_back(h_one_grad)
    input_grad = middle_grad + d_inputs
    grad_mod = jnp.concatenate(
        [d_shift_one, d_scale_one, d_gate_one, d_shift_two, d_scale_two, d_gate_two], axis=1
    ).astype(jnp.bfloat16)
    grad_ada = jnp.einsum("tc,tm->cm", cond_low, grad_mod, preferred_element_type=jnp.float32)
    bias_grad = jnp.sum(grad_mod.astype(jnp.float32), axis=0).reshape(6, model_width)
    grad_norm_rows = jnp.concatenate([d_gain_one[None], d_gain_two[None], bias_grad], axis=0)
    ada_sum, norm_sum, qkv_sum, out_sum, up_sum, down_sum = (
        lax.psum_scatter(grad_ada, "dp", scatter_dimension=1, tiled=True),
        lax.psum_scatter(grad_norm_rows, "dp", scatter_dimension=1, tiled=True),
        lax.psum_scatter(grad_qkv, "dp", scatter_dimension=1, tiled=True),
        lax.psum_scatter(grad_out, "dp", scatter_dimension=1, tiled=True),
        lax.psum_scatter(grad_up, "dp", scatter_dimension=0, tiled=True),
        lax.psum_scatter(grad_down, "dp", scatter_dimension=1, tiled=True),
    )
    token_total = float(tok_rows * lax.axis_size("dp"))
    ada_mean = ada_sum / token_total
    norm_mean = norm_sum / token_total
    qkv_mean = qkv_sum / token_total
    out_mean = out_sum / token_total
    up_mean = up_sum / token_total
    down_mean = down_sum / token_total
    shared_part = 1.0 / lax.axis_size("mp")
    local_sq = (
        jnp.sum(qkv_mean * qkv_mean)
        + jnp.sum(out_mean * out_mean)
        + jnp.sum(up_mean * up_mean)
        + jnp.sum(down_mean * down_mean)
        + shared_part * (jnp.sum(ada_mean * ada_mean) + jnp.sum(norm_mean * norm_mean))
    )
    total_sq = lax.psum(local_sq, ("dp", "mp"))
    grad_norm = jnp.sqrt(total_sq)
    clip_factor = jnp.minimum(1.0, clip_limit / (grad_norm + 1e-06))
    step_count = step[0].astype(jnp.float32)
    ada_new = adam_update(
        ada_weight,
        ada_first,
        ada_second,
        ada_mean,
        clip_factor,
        step_count,
        step_rates[0],
        decay_rates[0],
    )
    norm_new = adam_update(
        norm_params,
        norm_first,
        norm_second,
        norm_mean,
        clip_factor,
        step_count,
        step_rates[1],
        decay_rates[1],
    )
    qkv_new = adam_update(
        qkv_weight,
        qkv_first,
        qkv_second,
        qkv_mean,
        clip_factor,
        step_count,
        step_rates[2],
        decay_rates[2],
    )
    out_new = adam_update(
        out_weight,
        out_first,
        out_second,
        out_mean,
        clip_factor,
        step_count,
        step_rates[3],
        decay_rates[3],
    )
    up_new = adam_update(
        up_weight,
        up_first,
        up_second,
        up_mean,
        clip_factor,
        step_count,
        step_rates[4],
        decay_rates[4],
    )
    down_new = adam_update(
        down_weight,
        down_first,
        down_second,
        down_mean,
        clip_factor,
        step_count,
        step_rates[5],
        decay_rates[5],
    )
    return (
        result,
        input_grad,
        grad_norm.reshape(1),
        ada_new[0],
        ada_new[1],
        ada_new[2],
        norm_new[0],
        norm_new[1],
        norm_new[2],
        qkv_new[0],
        qkv_new[1],
        qkv_new[2],
        out_new[0],
        out_new[1],
        out_new[2],
        up_new[0],
        up_new[1],
        up_new[2],
        down_new[0],
        down_new[1],
        down_new[2],
    )


def solution(mesh):
    return jax.shard_map(
        per_device,
        mesh=mesh,
        in_specs=(
            P("dp", None),
            P("dp", None),
            P("dp", None),
            P("dp", None),
            P(),
            P(None, "dp"),
            P(None, "dp"),
            P(None, "dp"),
            P(None, "dp"),
            P(None, "dp"),
            P(None, "dp"),
            P(None, "dp", "mp"),
            P(None, "dp", "mp"),
            P(None, "dp", "mp"),
            P("mp", "dp"),
            P("mp", "dp"),
            P("mp", "dp"),
            P("dp", "mp"),
            P("dp", "mp"),
            P("dp", "mp"),
            P("mp", "dp"),
            P("mp", "dp"),
            P("mp", "dp"),
        ),
        out_specs=(
            P("dp", None),
            P("dp", None),
            P(),
            P(None, "dp"),
            P(None, "dp"),
            P(None, "dp"),
            P(None, "dp"),
            P(None, "dp"),
            P(None, "dp"),
            P(None, "dp", "mp"),
            P(None, "dp", "mp"),
            P(None, "dp", "mp"),
            P("mp", "dp"),
            P("mp", "dp"),
            P("mp", "dp"),
            P("dp", "mp"),
            P("dp", "mp"),
            P("dp", "mp"),
            P("mp", "dp"),
            P("mp", "dp"),
            P("mp", "dp"),
        ),
        check_vma=False,
    )
```

profile of v0, /device:TPU:0, one launch (start us, length us, event | category | flops | bytes accessed | tf_op | source)
XLA Modules:
  0.0 1853.0 jit_solution(10040764894950794897)
XLA Ops:
  16.6 42.8 %all-gather = bf16[16,48,8]{1,2,0:T(8,128)(2,1)S(1)} all-gather(bf16[1,48,8]{1,2,0:T(8,128)(2,1)S(1)} %convert_bitcast_fusion), channel_id=1, replica_groups=mesh['dp'=16,'mp'=2] {'dp'}, dimensions={0}, use_global_device_ids=true | all-gather | bytes 13056 | tf_op jit(solution)/shard_map/all_gather | solution.py:101
  60.7 43.1 %all_gather.21 = bf16[384,768]{0,1:T(8,128)(2,1)} all-gather(bf16[384,48]{0,1:T(8,128)(2,1)S(1)} %convert_element_type.96), channel_id=1, replica_groups=mesh['dp'=16,'mp'=2] {'dp'}, dimensions={1}, use_global_device_ids=true | all-gather | bytes 626688 | tf_op jit(solution)/shard_map/all_gather | solution.py:103
  103.8 16.4 convolution_add_fusion
  174.8 70.6 %while.26 = (s32[]{:T(128)}, bf16[2,1024,6,64]{1,3,2,0:T(8,128)(2,1)S(1)}, f32[2,6,1024,1]{2,1,3,0:T(8,128)S(1)}, bf16[2,1024,6,64]{1,3,2,0:T(8,128)(2,1)}, s32[...) while((s32[]{:T(128)}, ...), condition=%wide.region_5.6_spmd, body=%wide.region_2.5_spmd.sunk | while | flops 1681254400 | bytes 83089512 | solution.py:152
  255.9 28.3 %all-reduce.7.cloned.1.call-done = f32[2048,768]{1,0:T(8,128)} async-done(((f32[2048,768]{1,0:T(8,128)}), f32[2048,768]{1,0:T(8,128)}) %all-reduce.7.cloned.1.call-update) | async-done | bytes 6291472 | tf_op jit(solution)/shard_map/psum | solution.py:155
  299.2 52.1 %all-gather.10.cloned.1.call-done = bf16[768,1536]{1,0:T(8,128)(2,1)} async-done(((bf16[48,1536]{1,0:T(8,128)(2,1)}), bf16[768,1536]{1,0:T(8,128)(2,1)}) %all-gather.10.cloned.1.call-update) | async-done | bytes 2359312 | tf_op jit(solution)/shard_map/all_gather | solution.py:104
  351.3 13.0 multiply_convert_fusion.1
  364.3 51.7 %all-gather.12.cloned.1.call-done = bf16[1536,768]{0,1:T(8,128)(2,1)} async-done(((bf16[1536,48]{0,1:T(8,128)(2,1)}), bf16[1536,768]{0,1:T(8,128)(2,1)}) %all-gather.12.cloned.1.call-update) | async-done | bytes 2359312 | tf_op jit(solution)/shard_map/all_gather | solution.py:105
  416.0 15.9 fusion.94
  451.9 20.8 %all-reduce.9.cloned.1.call-done = f32[2048,768]{1,0:T(8,128)} async-done(((f32[2048,768]{1,0:T(8,128)}), f32[2048,768]{1,0:T(8,128)}) %all-reduce.9.cloned.1.call-update) | async-done | bytes 6291472 | tf_op jit(solution)/shard_map/psum | solution.py:172
  500.0 338.8 %while.27 = (s32[]{:T(128)}, f32[2,1024,6,64]{1,0,3,2:T(2,128)}, f32[2,1024,6,64]{1,0,3,2:T(2,128)}, bf16[2,1024,6,64]{1,3,2,0:T(8,128)(2,1)}, bf16[2,1024,6,64]...) while((s32[]{:T(128)}, f32[2,1024,6,64]{1,0,3,2:T(2,128)}, ...), condition=%wide.region_15.16_spmd, body=%wide.region_13.15_spmd.sunk | while | flops 4191172608 | bytes 306142336 | solution.py:207
  500.9 13.1 fusion.210
  526.5 13.1 fusion.209
  539.6 35.6 %fusion.212 = f32[1,1024,6,64]{1,3,2,0:T(8,128)} fusion(f32[6,1024,1024]{1,2,0:T(8,128)} %fusion.209, f32[6,1024,1024]{1,2,0:T(8,128)} %fusion.210, f32[6,1024]{1,0:T(8,128)S(1)} %dynamic-slice_bitcast_fusion.2, pred[1024,1024]{0,1:T(8,128)(4,1)S(1)} %broadcast_compare_fusion.5, bf16[2,1024,6,64]{1,3,2,0:T(8,128)(2,1)} %get-tuple-element.508, ...), kind=kOutput, calls=%fused_computation.45.clone.1 | convolution fusion | flops 874519552 | bytes 105185280 | tf_op jit(solution)/shard_map/while/body/eval_jaxpr/hqk,qhd->khd/dot_general | solution.py:202
  575.2 34.4 %fusion.211 = f32[1,1024,6,64]{1,3,2,0:T(8,128)S(1)} fusion(f32[6,1024,1024]{1,2,0:T(8,128)} %fusion.209, f32[6,1024,1024]{1,2,0:T(8,128)} %fusion.210, f32[6,1024]{1,0:T(8,128)S(1)} %dynamic-slice_bitcast_fusion.2, pred[1024,1024]{0,1:T(8,128)(4,1)S(1)} %broadcast_compare_fusion.5, bf16[2,1024,6,64]{1,3,2,0:T(8,128)(2,1)} %get-tuple-element.506, ...), kind=kOutput, calls=%fused_computation.44.clone.1 | convolution fusion | flops 874519552 | bytes 105185280 | tf_op jit(solution)/shard_map/while/body/eval_jaxpr/hqk,khd->qhd/dot_general | solution.py:199
  614.4 27.5 %dynamic_update_slice.30 = f32[2,1024,6,64]{1,0,3,2:T(2,128)} dynamic-update-slice(f32[2,1024,6,64]{1,0,3,2:T(2,128)} %get-tuple-element.492, f32[1,1024,6,64]{1,0,3,2:T(1,128)S(1)} %copy.200, s32[]{:T(128)S(6)} %copy.221, s32[]{:T(128)} %constant.54.clone.1..sunk, s32[]{:T(128)} %constant.54.clone.1..sunk, s32[]{:T(128)} %constant.54.clone.1..sunk) | dynamic-update-slice | bytes 3145732 | tf_op jit(solution)/shard_map/while/body/jit(dynamic_update_index_in_dim)/dynamic_update_slice | solution.py:207
  641.9 27.5 %dynamic_update_slice.29 = f32[2,1024,6,64]{1,0,3,2:T(2,128)} dynamic-update-slice(f32[2,1024,6,64]{1,0,3,2:T(2,128)} %get-tuple-element.491, f32[1,1024,6,64]{1,0,3,2:T(1,128)S(1)} %copy.199, s32[]{:T(128)S(6)} %copy.221, s32[]{:T(128)} %constant.54.clone.1..sunk, s32[]{:T(128)} %constant.54.clone.1..sunk, s32[]{:T(128)} %constant.54.clone.1..sunk) | dynamic-update-slice | bytes 3145732 | tf_op jit(solution)/shard_map/while/body/jit(dynamic_update_index_in_dim)/dynamic_update_slice | solution.py:207
  670.0 13.1 fusion.210
  695.6 13.1 fusion.209
  708.7 35.7 %fusion.212 = f32[1,1024,6,64]{1,3,2,0:T(8,128)} fusion(f32[6,1024,1024]{1,2,0:T(8,128)} %fusion.209, f32[6,1024,1024]{1,2,0:T(8,128)} %fusion.210, f32[6,1024]{1,0:T(8,128)S(1)} %dynamic-slice_bitcast_fusion.2, pred[1024,1024]{0,1:T(8,128)(4,1)S(1)} %broadcast_compare_fusion.5, bf16[2,1024,6,64]{1,3,2,0:T(8,128)(2,1)} %get-tuple-element.508, ...), kind=kOutput, calls=%fused_computation.45.clone.1 | convolution fusion | flops 874519552 | bytes 105185280 | tf_op jit(solution)/shard_map/while/body/eval_jaxpr/hqk,qhd->khd/dot_general | solution.py:202
  744.4 34.3 %fusion.211 = f32[1,1024,6,64]{1,3,2,0:T(8,128)S(1)} fusion(f32[6,1024,1024]{1,2,0:T(8,128)} %fusion.209, f32[6,1024,1024]{1,2,0:T(8,128)} %fusion.210, f32[6,1024]{1,0:T(8,128)S(1)} %dynamic-slice_bitcast_fusion.2, pred[1024,1024]{0,1:T(8,128)(4,1)S(1)} %broadcast_compare_fusion.5, bf16[2,1024,6,64]{1,3,2,0:T(8,128)(2,1)} %get-tuple-element.506, ...), kind=kOutput, calls=%fused_computation.44.clone.1 | convolution fusion | flops 874519552 | bytes 105185280 | tf_op jit(solution)/shard_map/while/body/eval_jaxpr/hqk,khd->qhd/dot_general | solution.py:199
  783.4 27.5 %dynamic_update_slice.30 = f32[2,1024,6,64]{1,0,3,2:T(2,128)} dynamic-update-slice(f32[2,1024,6,64]{1,0,3,2:T(2,128)} %get-tuple-element.492, f32[1,1024,6,64]{1,0,3,2:T(1,128)S(1)} %copy.200, s32[]{:T(128)S(6)} %copy.221, s32[]{:T(128)} %constant.54.clone.1..sunk, s32[]{:T(128)} %constant.54.clone.1..sunk, s32[]{:T(128)} %constant.54.clone.1..sunk) | dynamic-update-slice | bytes 3145732 | tf_op jit(solution)/shard_map/while/body/jit(dynamic_update_index_in_dim)/dynamic_update_slice | solution.py:207
  810.9 27.5 %dynamic_update_slice.29 = f32[2,1024,6,64]{1,0,3,2:T(2,128)} dynamic-update-slice(f32[2,1024,6,64]{1,0,3,2:T(2,128)} %get-tuple-element.491, f32[1,1024,6,64]{1,0,3,2:T(1,128)S(1)} %copy.199, s32[]{:T(128)S(6)} %copy.221, s32[]{:T(128)} %constant.54.clone.1..sunk, s32[]{:T(128)} %constant.54.clone.1..sunk, s32[]{:T(128)} %constant.54.clone.1..sunk) | dynamic-update-slice | bytes 3145732 | tf_op jit(solution)/shard_map/while/body/jit(dynamic_update_index_in_dim)/dynamic_update_slice | solution.py:207
  928.3 13.6 fusion.108
  974.5 12.6 fusion.135
  989.1 63.4 %reduce-scatter.8.cloned.1.call-done = f32[384,48]{0,1:T(8,128)} async-done(((f32[384,768]{0,1:T(8,128)}), f32[384,48]{0,1:T(8,128)}) %reduce-scatter.8.cloned.1.call-update) | async-done | bytes 73744 | tf_op jit(solution)/shard_map/reduce_scatter | solution.py:231
  1054.1 140.3 %reduce-scatter.10.cloned.1.call-done = f32[48,1536]{1,0:T(8,128)} async-done(((f32[768,1536]{1,0:T(8,128)}), f32[48,1536]{1,0:T(8,128)}) %reduce-scatter.10.cloned.1.call-update) | async-done | bytes 294928 | tf_op jit(solution)/shard_map/reduce_scatter | solution.py:232
  1196.0 141.0 %reduce-scatter.12.cloned.1.call-done = f32[1536,48]{0,1:T(8,128)} async-done(((f32[1536,768]{0,1:T(8,128)}), f32[1536,48]{0,1:T(8,128)}) %reduce-scatter.12.cloned.1.call-update) | async-done | bytes 294928 | tf_op jit(solution)/shard_map/reduce_scatter | solution.py:233
  1338.6 183.0 %all-reduce.11.cloned.1.call-done = f32[3,768,384]{2,0,1:T(4,128)} async-done(((f32[3,768,384]{2,0,1:T(4,128)}), f32[3,768,384]{2,0,1:T(4,128)}) %all-reduce.11.cloned.1.call-update) | async-done | bytes 3538960
  1527.1 120.3 %reduce-scatter.16.cloned.1.call-done = f32[48,8]{1,0:T(8,128)} async-done(((f32[768,8]{1,0:T(8,128)}), f32[48,8]{1,0:T(8,128)}) %reduce-scatter.16.cloned.1.call-update) | async-done | bytes 1552
  1648.8 130.9 %reduce-scatter.14.cloned.1.call-done = f32[128,288]{0,1:T(8,128)} async-done(((f32[128,4608]{0,1:T(8,128)}), f32[128,288]{0,1:T(8,128)}) %reduce-scatter.14.cloned.1.call-update) | async-done | bytes 147472 | tf_op jit(solution)/shard_map/reduce_scatter | solution.py:228
  1792.7 40.0 %psum.39 = f32[]{:T(128)} all-reduce(f32[]{:T(128)S(6)} %add.261), channel_id=1, replica_groups=mesh['dp'=16,'mp'=2] {'dp','mp'}, use_global_device_ids=true, to_apply=%region_34.35 | all-reduce | flops 1 | bytes 8 | tf_op jit(solution)/shard_map/psum | solution.py:250
  (267 shorter events, 398.3 us)
Async XLA Ops:
  7.2 52.3 %copy-start.27 = (f32[384,48]{0,1:T(8,128)S(1)}, f32[384,48]{0,1:T(8,128)}, u32[]{:S(2)}) copy-start(f32[384,48]{0,1:T(8,128)} %param.41) | copy-start | bytes 221188
  7.2 96.6 %all-gather.6.cloned.1.call-start = ((), (), s32[]{:S(2)}) async-start(), calls=%async_computation.5 | async-start | bytes 1253376 | tf_op jit(solution)/shard_map/all_gather | solution.py:100
  8.8 124.7 %all-gather.8.cloned.1.call-start = ((), (), s32[]{:S(2)}) async-start(), calls=%async_computation.6 | async-start | bytes 1880064 | tf_op jit(solution)/shard_map/all_gather | solution.py:102
  10.5 273.7 %all-reduce.7.cloned.1.call-start = ((), (), s32[]{:S(2)}) async-start(), calls=%async_computation.7 | async-start | bytes 12582912 | tf_op jit(solution)/shard_map/psum | solution.py:155
  13.6 106.6 %copy-start.23 = (f32[2048]{0:T(1024)}, f32[2048]{0:T(1024)S(1)}, u32[]{:S(2)}) copy-start(f32[2048]{0:T(1024)S(1)} %broadcast_multiply_fusion.1) | copy-start | bytes 24580
  16.6 44.1 %copy-start.40 = (f32[2048]{0:T(1024)}, f32[2048]{0:T(1024)S(1)}, u32[]{:S(2)}) copy-start(f32[2048]{0:T(1024)S(1)} %fusion.107) | copy-start | bytes 24580
  60.1 60.1 %copy-start.34 = (f32[768]{0:T(1024)}, f32[768]{0:T(1024)S(1)}, u32[]{:S(2)}) copy-start(f32[768]{0:T(1024)S(1)} %get-tuple-element.254) | copy-start | bytes 9220
  60.2 60.1 %copy-start.31 = (f32[2048]{0:T(1024)}, f32[2048]{0:T(1024)S(1)}, u32[]{:S(2)}) copy-start(f32[2048]{0:T(1024)S(1)} %fusion.130) | copy-start | bytes 24580
  60.7 100.9 %copy-start.17 = (f32[1024,32]{0,1:T(8,128)}, f32[1024,32]{0,1:T(8,128)S(1)}, u32[]{:S(2)}) copy-start(f32[1024,32]{0,1:T(8,128)S(1)} %get-tuple-element.336) | copy-start | bytes 393220
  60.7 100.9 %copy-start.19 = (f32[1024,32]{0,1:T(8,128)}, f32[1024,32]{0,1:T(8,128)S(1)}, u32[]{:S(2)}) copy-start(f32[1024,32]{0,1:T(8,128)S(1)} %get-tuple-element.337) | copy-start | bytes 393220
  103.8 16.4 copy-start.1
  253.2 31.0 %copy-start.2 = (bf16[2048,768]{1,0:T(8,128)(2,1)S(1)}, bf16[2048,768]{1,0:T(8,128)(2,1)}, u32[]{:S(2)}) copy-start(bf16[2048,768]{1,0:T(8,128)(2,1)} %param.27) | copy-start | bytes 9437188
  253.2 98.1 %all-gather.10.cloned.1.call-start = ((), (), s32[]{:S(2)}) async-start(), calls=%async_computation.8 | async-start | bytes 2506752 | tf_op jit(solution)/shard_map/all_gather | solution.py:104
  254.0 162.1 %all-gather.12.cloned.1.call-start = ((), (), s32[]{:S(2)}) async-start(), calls=%async_computation.9 | async-start | bytes 2506752 | tf_op jit(solution)/shard_map/all_gather | solution.py:105
  255.9 216.8 %all-reduce.9.cloned.1.call-start = ((), (), s32[]{:S(2)}) async-start(), calls=%async_computation.10 | async-start | bytes 12582912 | tf_op jit(solution)/shard_map/psum | solution.py:172
  289.7 191.3 %copy-start.25 = (f32[2048]{0:T(1024)}, f32[2048]{0:T(1024)S(1)}, u32[]{:S(2)}) copy-start(f32[2048]{0:T(1024)S(1)} %broadcast_multiply_fusion) | copy-start | bytes 24580
  290.6 190.4 %copy-start.29 = (f32[2048]{0:T(1024)}, f32[2048]{0:T(1024)S(1)}, u32[]{:S(2)}) copy-start(f32[2048]{0:T(1024)S(1)} %fusion.131) | copy-start | bytes 24580
  299.2 116.8 %copy-start.7 = (bf16[2048,768]{1,0:T(8,128)(2,1)S(1)}, bf16[2048,768]{1,0:T(8,128)(2,1)}, u32[]{:S(2)}) copy-start(bf16[2048,768]{1,0:T(8,128)(2,1)} %param.30) | copy-start | bytes 9437188
  416.0 18.6 %copy-start.43 = (bf16[768,1536]{1,0:T(8,128)(2,1)S(1)}, bf16[768,1536]{1,0:T(8,128)(2,1)}, u32[]{:S(2)}) copy-start(bf16[768,1536]{1,0:T(8,128)(2,1)} %all-gather.10.cloned.1.call-done) | copy-start | bytes 7077892
  441.6 480.6 %all-reduce.13.cloned.1.call-start = ((), (), s32[]{:S(2)}) async-start(), calls=%async_computation.17 | async-start | bytes 25165824 | tf_op jit(solution)/shard_map/psum | solution.py:162
  871.4 181.2 %reduce-scatter.8.cloned.1.call-start = ((), (), s32[]{:S(2)}) async-start(), calls=%async_computation.11 | async-start | bytes 1253376 | tf_op jit(solution)/shard_map/reduce_scatter | solution.py:231
  877.5 316.8 %reduce-scatter.10.cloned.1.call-start = ((), (), s32[]{:S(2)}) async-start(), calls=%async_computation.12 | async-start | bytes 5013504 | tf_op jit(solution)/shard_map/reduce_scatter | solution.py:232
  888.5 448.5 %reduce-scatter.12.cloned.1.call-start = ((), (), s32[]{:S(2)}) async-start(), calls=%async_computation.13 | async-start | bytes 5013504 | tf_op jit(solution)/shard_map/reduce_scatter | solution.py:233
  900.5 621.1 %all-reduce.11.cloned.1.call-start = ((), (), s32[]{:S(2)}) async-start(), calls=%async_computation.16 | async-start | bytes 9437184
  913.3 13.9 copy-start.24
  913.3 13.9 copy-start.35
  913.3 734.1 %reduce-scatter.16.cloned.1.call-start = ((), (), s32[]{:S(2)}) async-start(), calls=%async_computation.15 | async-start | bytes 417792
  942.0 16.1 slice-start.2
  974.2 808.4 %copy-start.4 = (bf16[2048,768]{1,0:T(8,128)(2,1)S(1)}, bf16[2048,768]{1,0:T(8,128)(2,1)}, u32[]{:S(2)}) copy-start(bf16[2048,768]{1,0:T(8,128)(2,1)} %param.27) | copy-start | bytes 9437188
  974.2 805.6 %reduce-scatter.14.cloned.1.call-start = ((), (), s32[]{:S(2)}) async-start(), calls=%async_computation.14 | async-start | bytes 2506752 | tf_op jit(solution)/shard_map/reduce_scatter | solution.py:228
  1782.6 54.4 %copy-start.28 = (f32[384,48]{0,1:T(8,128)S(1)}, f32[384,48]{0,1:T(8,128)}, u32[]{:S(2)}) copy-start(f32[384,48]{0,1:T(8,128)} %param.41) | copy-start | bytes 221188
  1782.6 58.0 %copy-start.22 = (f32[48,1536]{1,0:T(8,128)S(1)}, f32[48,1536]{1,0:T(8,128)}, u32[]{:S(2)}) copy-start(f32[48,1536]{1,0:T(8,128)} %param.44) | copy-start | bytes 884740
  (35 other events, 229.2 us)
Sparse Core Ops, SparseCore 0:
  11.4 59.7 all-gather.5
  74.5 58.9 all-gather.7
  253.3 30.7 all-reduce.6
  287.8 63.4 all-gather.9
  354.9 61.0 all-gather.11
  441.7 30.8 all-reduce.8
  871.5 50.6 all-reduce.12
  927.0 125.5 reduce-scatter.7
  1057.8 136.5 reduce-scatter.9
  1200.2 136.7 reduce-scatter.11
  1342.7 178.8 all-reduce.10
  1526.8 120.5 reduce-scatter.15
  1652.3 127.3 reduce-scatter.13
where the time goes:
time: 1860 us; the launch traced here: 1850 us
  waiting for transfers between devices  947 us (51%)
  matrix products  399 us (21%)
  other arithmetic  180 us (10%)
  local copies, waits for them, and re-layouts  178 us (10%)
  blocking collectives  126 us (7%)
  between operations  22.2 us (1%)
    unnamed x15, waiting for transfers between devices  303 us
    reduce_scatter x1, waiting for transfers between devices, per_device(): lax.psum_scatter(grad_down, 'dp', scatter_dimension=1, tiled=True)  141 us
    reduce_scatter x1, waiting for transfers between devices, per_device(): lax.psum_scatter(grad_up, 'dp', scatter_dimension=0, tiled=True)  140 us
    reduce_scatter x1, waiting for transfers between devices, per_device(): lax.psum_scatter(grad_ada, 'dp', scatter_dimension=1, tiled=True)  131 us
    dynamic_update_slice x8, local copies, waits for them, and re-layouts, per_device(): lax.map(attend_back, (queries, keys, values, segments, logsums, grad_atte...  119 us
    dot_general x2, matrix products, attend_back(): jnp.einsum('hqk,qhd->khd', grad_scores, query_block, preferred_element_ty...  71.3 us
    dot_general x2, matrix products, attend_back(): jnp.einsum('hqk,khd->qhd', grad_scores, key_block, preferred_element_type...  68.8 us
    reduce_scatter x1, waiting for transfers between devices, per_device(): lax.psum_scatter(grad_out, 'dp', scatter_dimension=1, tiled=True)  63.4 us
  transfers between devices with their start and end apart: 13, of which 12 were waited for; matrix products, arithmetic and copies ran while one was open for 10% of the time, Pallas kernels for 0%

commit v1 on v0

--- a/solution.py
+++ b/solution.py
@@ -247,7 +247,8 @@
         + jnp.sum(down_mean * down_mean)
         + shared_part * (jnp.sum(ada_mean * ada_mean) + jnp.sum(norm_mean * norm_mean))
     )
-    total_sq = lax.psum(local_sq, ("dp", "mp"))
+    parts = lax.all_gather(local_sq, ("dp", "mp"))
+    total_sq = jnp.sum(parts, axis=0)
     grad_norm = jnp.sqrt(total_sq)
     clip_factor = jnp.minimum(1.0, clip_limit / (grad_norm + 1e-06))
     step_count = step[0].astype(jnp.float32)

time: 1860 us -> 1870 us (level)
    unnamed x0 -> x1, blocking collectives: none -> 40.3 us
    psum x1 -> x0, blocking collectives: 40 us -> none  [per_device(): total_sq = lax.psum(local_sq, ('dp', 'mp'))]
where the time goes in v1:
time: 1870 us; the launch traced here: 1860 us
  waiting for transfers between devices  947 us (51%)
  matrix products  399 us (21%)
  other arithmetic  181 us (10%)
  local copies, waits for them, and re-layouts  180 us (10%)
  blocking collectives  126 us (7%)
  between operations  22.2 us (1%)
    unnamed x15, waiting for transfers between devices  304 us
    reduce_scatter x1, waiting for transfers between devices, per_device(): lax.psum_scatter(grad_down, 'dp', scatter_dimension=1, tiled=True)  141 us
    reduce_scatter x1, waiting for transfers between devices, per_device(): lax.psum_scatter(grad_up, 'dp', scatter_dimension=0, tiled=True)  140 us
    reduce_scatter x1, waiting for transfers between devices, per_device(): lax.psum_scatter(grad_ada, 'dp', scatter_dimension=1, tiled=True)  131 us
    dynamic_update_slice x8, local copies, waits for them, and re-layouts, per_device(): lax.map(attend_back, (queries, keys, values, segments, logsums, grad_atte...  120 us
    dot_general x2, matrix products, attend_back(): jnp.einsum('hqk,qhd->khd', grad_scores, query_block, preferred_element_ty...  71.4 us
    dot_general x2, matrix products, attend_back(): jnp.einsum('hqk,khd->qhd', grad_scores, key_block, preferred_element_type...  68.8 us
    reduce_scatter x1, waiting for transfers between devices, per_device(): lax.psum_scatter(grad_out, 'dp', scatter_dimension=1, tiled=True)  63.2 us
  transfers between devices with their start and end apart: 13, of which 12 were waited for; matrix products, arithmetic and copies ran while one was open for 10% of the time, Pallas kernels for 0%

profile of v1, /device:TPU:0, one launch (start us, length us, event | category | flops | bytes accessed | tf_op | source)
XLA Modules:
  0.0 1856.1 jit_solution(2001908157346540740)
XLA Ops:
  16.6 42.8 %all-gather = bf16[16,48,8]{1,2,0:T(8,128)(2,1)S(1)} all-gather(bf16[1,48,8]{1,2,0:T(8,128)(2,1)S(1)} %convert_bitcast_fusion), channel_id=1, replica_groups=mesh['dp'=16,'mp'=2] {'dp'}, dimensions={0}, use_global_device_ids=true | all-gather | bytes 13056 | tf_op jit(solution)/shard_map/all_gather | solution.py:101
  60.7 43.1 %all_gather.27 = bf16[384,768]{0,1:T(8,128)(2,1)} all-gather(bf16[384,48]{0,1:T(8,128)(2,1)S(1)} %convert_element_type.96), channel_id=1, replica_groups=mesh['dp'=16,'mp'=2] {'dp'}, dimensions={1}, use_global_device_ids=true | all-gather | bytes 626688 | tf_op jit(solution)/shard_map/all_gather | solution.py:103
  103.8 16.3 convolution_add_fusion
  174.9 70.6 %while.26 = (s32[]{:T(128)}, bf16[2,1024,6,64]{1,3,2,0:T(8,128)(2,1)S(1)}, f32[2,6,1024,1]{2,1,3,0:T(8,128)S(1)}, bf16[2,1024,6,64]{1,3,2,0:T(8,128)(2,1)}, s32[...) while((s32[]{:T(128)}, ...), condition=%wide.region_5.6_spmd, body=%wide.region_2.5_spmd.sunk | while | flops 1681254400 | bytes 83089512 | solution.py:152
  255.9 28.3 %all-reduce.8.cloned.1.call-done = f32[2048,768]{1,0:T(8,128)} async-done(((f32[2048,768]{1,0:T(8,128)}), f32[2048,768]{1,0:T(8,128)}) %all-reduce.8.cloned.1.call-update) | async-done | bytes 6291472 | tf_op jit(solution)/shard_map/psum | solution.py:155
  299.5 51.9 %all-gather.10.cloned.1.call-done = bf16[768,1536]{1,0:T(8,128)(2,1)} async-done(((bf16[48,1536]{1,0:T(8,128)(2,1)}), bf16[768,1536]{1,0:T(8,128)(2,1)}) %all-gather.10.cloned.1.call-update) | async-done | bytes 2359312 | tf_op jit(solution)/shard_map/all_gather | solution.py:104
  351.3 13.0 multiply_convert_fusion.1
  364.4 51.7 %all-gather.12.cloned.1.call-done = bf16[1536,768]{0,1:T(8,128)(2,1)} async-done(((bf16[1536,48]{0,1:T(8,128)(2,1)}), bf16[1536,768]{0,1:T(8,128)(2,1)}) %all-gather.12.cloned.1.call-update) | async-done | bytes 2359312 | tf_op jit(solution)/shard_map/all_gather | solution.py:105
  416.1 16.0 fusion.94
  452.0 20.8 %all-reduce.10.cloned.1.call-done = f32[2048,768]{1,0:T(8,128)} async-done(((f32[2048,768]{1,0:T(8,128)}), f32[2048,768]{1,0:T(8,128)}) %all-reduce.10.cloned.1.call-update) | async-done | bytes 6291472 | tf_op jit(solution)/shard_map/psum | solution.py:172
  500.2 339.3 %while.27 = (s32[]{:T(128)}, f32[2,1024,6,64]{1,0,3,2:T(2,128)}, f32[2,1024,6,64]{1,0,3,2:T(2,128)}, bf16[2,1024,6,64]{1,3,2,0:T(8,128)(2,1)}, bf16[2,1024,6,64]...) while((s32[]{:T(128)}, f32[2,1024,6,64]{1,0,3,2:T(2,128)}, ...), condition=%wide.region_15.16_spmd, body=%wide.region_13.15_spmd.sunk | while | flops 4191172608 | bytes 306142336 | solution.py:207
  501.1 13.1 fusion.210
  526.7 13.1 fusion.209
  539.8 35.6 %fusion.212 = f32[1,1024,6,64]{1,3,2,0:T(8,128)} fusion(f32[6,1024,1024]{1,2,0:T(8,128)} %fusion.209, f32[6,1024,1024]{1,2,0:T(8,128)} %fusion.210, f32[6,1024]{1,0:T(8,128)S(1)} %dynamic-slice_bitcast_fusion.2, pred[1024,1024]{0,1:T(8,128)(4,1)S(1)} %broadcast_compare_fusion.5, bf16[2,1024,6,64]{1,3,2,0:T(8,128)(2,1)} %get-tuple-element.508, ...), kind=kOutput, calls=%fused_computation.45.clone.1 | convolution fusion | flops 874519552 | bytes 105185280 | tf_op jit(solution)/shard_map/while/body/eval_jaxpr/hqk,qhd->khd/dot_general | solution.py:202
  575.4 34.5 %fusion.211 = f32[1,1024,6,64]{1,3,2,0:T(8,128)S(1)} fusion(f32[6,1024,1024]{1,2,0:T(8,128)} %fusion.209, f32[6,1024,1024]{1,2,0:T(8,128)} %fusion.210, f32[6,1024]{1,0:T(8,128)S(1)} %dynamic-slice_bitcast_fusion.2, pred[1024,1024]{0,1:T(8,128)(4,1)S(1)} %broadcast_compare_fusion.5, bf16[2,1024,6,64]{1,3,2,0:T(8,128)(2,1)} %get-tuple-element.506, ...), kind=kOutput, calls=%fused_computation.44.clone.1 | convolution fusion | flops 874519552 | bytes 105185280 | tf_op jit(solution)/shard_map/while/body/eval_jaxpr/hqk,khd->qhd/dot_general | solution.py:199
  614.6 27.6 %dynamic_update_slice.30 = f32[2,1024,6,64]{1,0,3,2:T(2,128)} dynamic-update-slice(f32[2,1024,6,64]{1,0,3,2:T(2,128)} %get-tuple-element.492, f32[1,1024,6,64]{1,0,3,2:T(1,128)S(1)} %copy.201, s32[]{:T(128)S(6)} %copy.222, s32[]{:T(128)} %constant.54.clone.1..sunk, s32[]{:T(128)} %constant.54.clone.1..sunk, s32[]{:T(128)} %constant.54.clone.1..sunk) | dynamic-update-slice | bytes 3145732 | tf_op jit(solution)/shard_map/while/body/jit(dynamic_update_index_in_dim)/dynamic_update_slice | solution.py:207
  642.2 27.6 %dynamic_update_slice.29 = f32[2,1024,6,64]{1,0,3,2:T(2,128)} dynamic-update-slice(f32[2,1024,6,64]{1,0,3,2:T(2,128)} %get-tuple-element.491, f32[1,1024,6,64]{1,0,3,2:T(1,128)S(1)} %copy.200, s32[]{:T(128)S(6)} %copy.222, s32[]{:T(128)} %constant.54.clone.1..sunk, s32[]{:T(128)} %constant.54.clone.1..sunk, s32[]{:T(128)} %constant.54.clone.1..sunk) | dynamic-update-slice | bytes 3145732 | tf_op jit(solution)/shard_map/while/body/jit(dynamic_update_index_in_dim)/dynamic_update_slice | solution.py:207
  670.5 13.1 fusion.210
  696.0 13.1 fusion.209
  709.2 35.7 %fusion.212 = f32[1,1024,6,64]{1,3,2,0:T(8,128)} fusion(f32[6,1024,1024]{1,2,0:T(8,128)} %fusion.209, f32[6,1024,1024]{1,2,0:T(8,128)} %fusion.210, f32[6,1024]{1,0:T(8,128)S(1)} %dynamic-slice_bitcast_fusion.2, pred[1024,1024]{0,1:T(8,128)(4,1)S(1)} %broadcast_compare_fusion.5, bf16[2,1024,6,64]{1,3,2,0:T(8,128)(2,1)} %get-tuple-element.508, ...), kind=kOutput, calls=%fused_computation.45.clone.1 | convolution fusion | flops 874519552 | bytes 105185280 | tf_op jit(solution)/shard_map/while/body/eval_jaxpr/hqk,qhd->khd/dot_general | solution.py:202
  744.9 34.4 %fusion.211 = f32[1,1024,6,64]{1,3,2,0:T(8,128)S(1)} fusion(f32[6,1024,1024]{1,2,0:T(8,128)} %fusion.209, f32[6,1024,1024]{1,2,0:T(8,128)} %fusion.210, f32[6,1024]{1,0:T(8,128)S(1)} %dynamic-slice_bitcast_fusion.2, pred[1024,1024]{0,1:T(8,128)(4,1)S(1)} %broadcast_compare_fusion.5, bf16[2,1024,6,64]{1,3,2,0:T(8,128)(2,1)} %get-tuple-element.506, ...), kind=kOutput, calls=%fused_computation.44.clone.1 | convolution fusion | flops 874519552 | bytes 105185280 | tf_op jit(solution)/shard_map/while/body/eval_jaxpr/hqk,khd->qhd/dot_general | solution.py:199
  784.0 27.6 %dynamic_update_slice.30 = f32[2,1024,6,64]{1,0,3,2:T(2,128)} dynamic-update-slice(f32[2,1024,6,64]{1,0,3,2:T(2,128)} %get-tuple-element.492, f32[1,1024,6,64]{1,0,3,2:T(1,128)S(1)} %copy.201, s32[]{:T(128)S(6)} %copy.222, s32[]{:T(128)} %constant.54.clone.1..sunk, s32[]{:T(128)} %constant.54.clone.1..sunk, s32[]{:T(128)} %constant.54.clone.1..sunk) | dynamic-update-slice | bytes 3145732 | tf_op jit(solution)/shard_map/while/body/jit(dynamic_update_index_in_dim)/dynamic_update_slice | solution.py:207
  811.6 27.6 %dynamic_update_slice.29 = f32[2,1024,6,64]{1,0,3,2:T(2,128)} dynamic-update-slice(f32[2,1024,6,64]{1,0,3,2:T(2,128)} %get-tuple-element.491, f32[1,1024,6,64]{1,0,3,2:T(1,128)S(1)} %copy.200, s32[]{:T(128)S(6)} %copy.222, s32[]{:T(128)} %constant.54.clone.1..sunk, s32[]{:T(128)} %constant.54.clone.1..sunk, s32[]{:T(128)} %constant.54.clone.1..sunk) | dynamic-update-slice | bytes 3145732 | tf_op jit(solution)/shard_map/while/body/jit(dynamic_update_index_in_dim)/dynamic_update_slice | solution.py:207
  929.1 13.6 fusion.108
  975.6 12.6 fusion.135
  990.2 63.2 %reduce-scatter.8.cloned.1.call-done = f32[384,48]{0,1:T(8,128)} async-done(((f32[384,768]{0,1:T(8,128)}), f32[384,48]{0,1:T(8,128)}) %reduce-scatter.8.cloned.1.call-update) | async-done | bytes 73744 | tf_op jit(solution)/shard_map/reduce_scatter | solution.py:231
  1054.9 140.2 %reduce-scatter.10.cloned.1.call-done = f32[48,1536]{1,0:T(8,128)} async-done(((f32[768,1536]{1,0:T(8,128)}), f32[48,1536]{1,0:T(8,128)}) %reduce-scatter.10.cloned.1.call-update) | async-done | bytes 294928 | tf_op jit(solution)/shard_map/reduce_scatter | solution.py:232
  1196.8 140.7 %reduce-scatter.12.cloned.1.call-done = f32[1536,48]{0,1:T(8,128)} async-done(((f32[1536,768]{0,1:T(8,128)}), f32[1536,48]{0,1:T(8,128)}) %reduce-scatter.12.cloned.1.call-update) | async-done | bytes 294928 | tf_op jit(solution)/shard_map/reduce_scatter | solution.py:233
  1339.1 183.0 %all-reduce.12.cloned.1.call-done = f32[3,768,384]{2,0,1:T(4,128)} async-done(((f32[3,768,384]{2,0,1:T(4,128)}), f32[3,768,384]{2,0,1:T(4,128)}) %all-reduce.12.cloned.1.call-update) | async-done | bytes 3538960
  1527.7 120.3 %reduce-scatter.16.cloned.1.call-done = f32[48,8]{1,0:T(8,128)} async-done(((f32[768,8]{1,0:T(8,128)}), f32[48,8]{1,0:T(8,128)}) %reduce-scatter.16.cloned.1.call-update) | async-done | bytes 1552
  1649.4 130.9 %reduce-scatter.14.cloned.1.call-done = f32[128,288]{0,1:T(8,128)} async-done(((f32[128,4608]{0,1:T(8,128)}), f32[128,288]{0,1:T(8,128)}) %reduce-scatter.14.cloned.1.call-update) | async-done | bytes 147472 | tf_op jit(solution)/shard_map/reduce_scatter | solution.py:228
  1795.0 40.3 %all-reduce = f32[32]{0:T(128)S(1)} all-reduce(f32[32]{0:T(128)} %dynamic-update-slice), channel_id=1, replica_groups=mesh['dp'=16,'mp'=2] {'dp','mp'}, use_global_device_ids=true, to_apply=%add | all-reduce | flops 32 | bytes 256
  (270 shorter events, 401.4 us)
Async XLA Ops:
  7.2 52.3 %copy-start.27 = (f32[384,48]{0,1:T(8,128)S(1)}, f32[384,48]{0,1:T(8,128)}, u32[]{:S(2)}) copy-start(f32[384,48]{0,1:T(8,128)} %param.41) | copy-start | bytes 221188
  7.2 96.6 %all-gather.6.cloned.1.call-start = ((), (), s32[]{:S(2)}) async-start(), calls=%async_computation.5 | async-start | bytes 1253376 | tf_op jit(solution)/shard_map/all_gather | solution.py:100
  8.8 124.7 %all-gather.8.cloned.1.call-start = ((), (), s32[]{:S(2)}) async-start(), calls=%async_computation.6 | async-start | bytes 1880064 | tf_op jit(solution)/shard_map/all_gather | solution.py:102
  10.5 273.7 %all-reduce.8.cloned.1.call-start = ((), (), s32[]{:S(2)}) async-start(), calls=%async_computation.7 | async-start | bytes 12582912 | tf_op jit(solution)/shard_map/psum | solution.py:155
  13.6 106.5 %copy-start.23 = (f32[2048]{0:T(1024)}, f32[2048]{0:T(1024)S(1)}, u32[]{:S(2)}) copy-start(f32[2048]{0:T(1024)S(1)} %broadcast_multiply_fusion.1) | copy-start | bytes 24580
  16.6 44.1 %copy-start.40 = (f32[2048]{0:T(1024)}, f32[2048]{0:T(1024)S(1)}, u32[]{:S(2)}) copy-start(f32[2048]{0:T(1024)S(1)} %fusion.107) | copy-start | bytes 24580
  60.1 60.0 %copy-start.34 = (f32[768]{0:T(1024)}, f32[768]{0:T(1024)S(1)}, u32[]{:S(2)}) copy-start(f32[768]{0:T(1024)S(1)} %get-tuple-element.254) | copy-start | bytes 9220
  60.2 60.0 %copy-start.31 = (f32[2048]{0:T(1024)}, f32[2048]{0:T(1024)S(1)}, u32[]{:S(2)}) copy-start(f32[2048]{0:T(1024)S(1)} %fusion.130) | copy-start | bytes 24580
  60.7 100.9 %copy-start.17 = (f32[1024,32]{0,1:T(8,128)}, f32[1024,32]{0,1:T(8,128)S(1)}, u32[]{:S(2)}) copy-start(f32[1024,32]{0,1:T(8,128)S(1)} %get-tuple-element.336) | copy-start | bytes 393220
  60.7 100.9 %copy-start.19 = (f32[1024,32]{0,1:T(8,128)}, f32[1024,32]{0,1:T(8,128)S(1)}, u32[]{:S(2)}) copy-start(f32[1024,32]{0,1:T(8,128)S(1)} %get-tuple-element.337) | copy-start | bytes 393220
  103.8 16.3 copy-start.1
  253.2 31.0 %copy-start.2 = (bf16[2048,768]{1,0:T(8,128)(2,1)S(1)}, bf16[2048,768]{1,0:T(8,128)(2,1)}, u32[]{:S(2)}) copy-start(bf16[2048,768]{1,0:T(8,128)(2,1)} %param.27) | copy-start | bytes 9437188
  253.3 98.1 %all-gather.10.cloned.1.call-start = ((), (), s32[]{:S(2)}) async-start(), calls=%async_computation.8 | async-start | bytes 2506752 | tf_op jit(solution)/shard_map/all_gather | solution.py:104
  254.0 162.0 %all-gather.12.cloned.1.call-start = ((), (), s32[]{:S(2)}) async-start(), calls=%async_computation.9 | async-start | bytes 2506752 | tf_op jit(solution)/shard_map/all_gather | solution.py:105
  255.9 216.9 %all-reduce.10.cloned.1.call-start = ((), (), s32[]{:S(2)}) async-start(), calls=%async_computation.10 | async-start | bytes 12582912 | tf_op jit(solution)/shard_map/psum | solution.py:172
  289.9 191.2 %copy-start.25 = (f32[2048]{0:T(1024)}, f32[2048]{0:T(1024)S(1)}, u32[]{:S(2)}) copy-start(f32[2048]{0:T(1024)S(1)} %broadcast_multiply_fusion) | copy-start | bytes 24580
  290.8 190.3 %copy-start.29 = (f32[2048]{0:T(1024)}, f32[2048]{0:T(1024)S(1)}, u32[]{:S(2)}) copy-start(f32[2048]{0:T(1024)S(1)} %fusion.131) | copy-start | bytes 24580
  299.5 116.6 %copy-start.7 = (bf16[2048,768]{1,0:T(8,128)(2,1)S(1)}, bf16[2048,768]{1,0:T(8,128)(2,1)}, u32[]{:S(2)}) copy-start(bf16[2048,768]{1,0:T(8,128)(2,1)} %param.30) | copy-start | bytes 9437188
  416.1 18.7 %copy-start.43 = (bf16[768,1536]{1,0:T(8,128)(2,1)S(1)}, bf16[768,1536]{1,0:T(8,128)(2,1)}, u32[]{:S(2)}) copy-start(bf16[768,1536]{1,0:T(8,128)(2,1)} %all-gather.10.cloned.1.call-done) | copy-start | bytes 7077892
  441.8 481.3 %all-reduce.14.cloned.1.call-start = ((), (), s32[]{:S(2)}) async-start(), calls=%async_computation.17 | async-start | bytes 25165824 | tf_op jit(solution)/shard_map/psum | solution.py:162
  872.2 181.2 %reduce-scatter.8.cloned.1.call-start = ((), (), s32[]{:S(2)}) async-start(), calls=%async_computation.11 | async-start | bytes 1253376 | tf_op jit(solution)/shard_map/reduce_scatter | solution.py:231
  878.4 316.8 %reduce-scatter.10.cloned.1.call-start = ((), (), s32[]{:S(2)}) async-start(), calls=%async_computation.12 | async-start | bytes 5013504 | tf_op jit(solution)/shard_map/reduce_scatter | solution.py:232
  889.3 448.2 %reduce-scatter.12.cloned.1.call-start = ((), (), s32[]{:S(2)}) async-start(), calls=%async_computation.13 | async-start | bytes 5013504 | tf_op jit(solution)/shard_map/reduce_scatter | solution.py:233
  901.3 620.8 %all-reduce.12.cloned.1.call-start = ((), (), s32[]{:S(2)}) async-start(), calls=%async_computation.16 | async-start | bytes 9437184
  914.1 13.9 copy-start.24
  914.1 13.9 copy-start.35
  914.1 733.9 %reduce-scatter.16.cloned.1.call-start = ((), (), s32[]{:S(2)}) async-start(), calls=%async_computation.15 | async-start | bytes 417792
  942.8 16.1 slice-start.2
  975.3 809.7 %copy-start.4 = (bf16[2048,768]{1,0:T(8,128)(2,1)S(1)}, bf16[2048,768]{1,0:T(8,128)(2,1)}, u32[]{:S(2)}) copy-start(bf16[2048,768]{1,0:T(8,128)(2,1)} %param.27) | copy-start | bytes 9437188
  975.3 805.1 %reduce-scatter.14.cloned.1.call-start = ((), (), s32[]{:S(2)}) async-start(), calls=%async_computation.14 | async-start | bytes 2506752 | tf_op jit(solution)/shard_map/reduce_scatter | solution.py:228
  1785.0 55.2 %copy-start.28 = (f32[384,48]{0,1:T(8,128)S(1)}, f32[384,48]{0,1:T(8,128)}, u32[]{:S(2)}) copy-start(f32[384,48]{0,1:T(8,128)} %param.41) | copy-start | bytes 221188
  1785.0 58.8 %copy-start.22 = (f32[48,1536]{1,0:T(8,128)S(1)}, f32[48,1536]{1,0:T(8,128)}, u32[]{:S(2)}) copy-start(f32[48,1536]{1,0:T(8,128)} %param.44) | copy-start | bytes 884740
  (35 other events, 229.4 us)
Sparse Core Ops, SparseCore 0:
  11.4 59.7 all-gather.5
  74.5 58.9 all-gather.7
  253.4 30.7 all-reduce.7
  287.8 63.4 all-gather.9
  354.9 61.0 all-gather.11
  441.9 30.8 all-reduce.9
  872.3 50.6 all-reduce.13
  927.8 125.5 reduce-scatter.7
  1058.6 136.4 reduce-scatter.9
  1201.0 136.4 reduce-scatter.11
  1343.2 178.8 all-reduce.11
  1527.4 120.5 reduce-scatter.15
  1652.9 127.3 reduce-scatter.13
